TPU v7x, 256 devices: a whole 4x4x8 slice. The times are simulated.
256 devices in a mesh: leaf: 16 (over y, x), row: 16 (over z, core).
Axes of the slice: x: 4, y: 4, z: 8, core: 2. Of those that a mesh axis runs over, the one named last changes fastest.
Arguments:
- sigma_root: float32 [2048, 2048], P(None, 'row')
- linv_one: bfloat16 [16, 2048, 2048], P('leaf', None, 'row'), as said below
- panel_one: bfloat16 [16, 512, 2048], P('leaf', None, 'row'), may hold values from -1.25 to 1.25
- tiles_one: int32 [16, 4], replicated, may hold values from 0 to 15, as said below
- mask_one: int32 [16, 4, 16], P('leaf', None, 'row'), may hold values 0 or 1
- linv_two: bfloat16 [16, 2048, 2048], P('leaf', None, 'row'), as said below
- panel_two: bfloat16 [16, 512, 2048], P('leaf', None, 'row'), may hold values from -1.25 to 1.25
- tiles_two: int32 [16, 4], replicated, may hold values from 0 to 15, as said below
- mask_two: int32 [16, 4, 16], P('leaf', None, 'row'), may hold values 0 or 1
- parent: int32 [16], replicated, may hold values from 0 to 15
Outputs:
- sigma_one: float32 [16, 2048, 2048], P('leaf', None, 'row')
- cross_one: float32 [16, 512, 2048], P('leaf', None, 'row')
- sigma_two: float32 [16, 2048, 2048], P('leaf', None, 'row')
- cross_two: float32 [16, 512, 2048], P('leaf', None, 'row')
Inputs may be any that keep to these rules, and one draw needn't show every extreme that they name: `tiles_one`: each row holds 4 different tile numbers in increasing order. `tiles_two`: each row holds 4 different tile numbers in increasing order. `linv_one`: each block is lower triangular with a positive diagonal. `sigma_root`: symmetric. `linv_two`: each block is lower triangular with a positive diagonal.
All inputs are finite; a program needn't handle non-finite values. No bound on the sum of `mask_one` or of `mask_two` on one device may be relied on, other than what follows from the above.
Results may differ from a plain program's by a relative error of at most 0.00045.
Values may be sent and summed in bfloat16 or wider, within the bound.
No kernel may reach another device: no remote copies, remote signals or barrier semaphores. Data moves between devices by JAX's collectives and lax.ppermute only.
A program may use at most 64 MiB of HBM per device.

v0:
```python
import jax
import jax.numpy as jnp
from jax import lax
from jax.sharding import PartitionSpec as P

TILE = 128


def pattern_rows(tile_list):
    offsets = jnp.arange(TILE, dtype=jnp.int32)
    return (tile_list[..., None] * TILE + offsets).reshape(tile_list.shape[:-1] + (-1,))


def expand_mask(tile_mask):
    return jnp.repeat(jnp.repeat(tile_mask, TILE, axis=0), TILE, axis=1)


def assemble(selected, row_list):
    gathered = lax.all_gather(selected, "row", axis=1, tiled=True)
    return jnp.take(gathered, row_list, axis=1)


def solve_block(selected, row_list, linv_local, panel_local, mask_local):
    select = assemble(selected, row_list)
    masked = panel_local * expand_mask(mask_local).astype(jnp.bfloat16)
    linv_wide = linv_local.astype(jnp.float32)
    whole_panel = lax.all_gather(masked, "row", axis=1, tiled=True)
    upper_part = jnp.dot(whole_panel, linv_local, preferred_element_type=jnp.float32)
    cross = -jnp.dot(select, upper_part, precision=lax.Precision.HIGHEST)
    middle = linv_wide - jnp.dot(
        whole_panel.astype(jnp.float32).T, cross, precision=lax.Precision.HIGHEST
    )
    sigma = jnp.dot(
        lax.all_gather(linv_local, "row", axis=1, tiled=True).astype(jnp.float32).T,
        middle,
        precision=lax.Precision.HIGHEST,
    )
    return (sigma, cross)


def body(
    sigma_root,
    linv_one,
    panel_one,
    tiles_one,
    mask_one,
    linv_two,
    panel_two,
    tiles_two,
    mask_two,
    parent,
):
    leaf_id = lax.axis_index("leaf")
    width = sigma_root.shape[1]
    own_tiles = lax.dynamic_index_in_dim(tiles_one, leaf_id, 0, keepdims=False)
    rows_first = pattern_rows(own_tiles)
    selected_first = jnp.take(sigma_root, rows_first, axis=0)
    sigma_first, cross_first = solve_block(
        selected_first, rows_first, linv_one[0], panel_one[0], mask_one[0]
    )
    rows_every = pattern_rows(tiles_two)
    count = rows_every.shape[0]
    block_rows = rows_every.shape[1]
    owned = (parent == leaf_id).astype(jnp.float32)
    slots = jnp.take(sigma_first, rows_every.reshape(-1), axis=0).reshape(count, block_rows, width)
    slots = slots * owned[:, None, None]
    arrived = lax.all_to_all(slots, "leaf", split_axis=0, concat_axis=0, tiled=True)
    selected_second = jnp.sum(arrived, axis=0)
    rows_second = lax.dynamic_index_in_dim(rows_every, leaf_id, 0, keepdims=False)
    sigma_second, cross_second = solve_block(
        selected_second, rows_second, linv_two[0], panel_two[0], mask_two[0]
    )
    return (sigma_first[None], cross_first[None], sigma_second[None], cross_second[None])


def solution(mesh):
    return jax.shard_map(
        body,
        mesh=mesh,
        in_specs=(
            P(None, "row"),
            P("leaf", None, "row"),
            P("leaf", None, "row"),
            P(),
            P("leaf", None, "row"),
            P("leaf", None, "row"),
            P("leaf", None, "row"),
            P(),
            P("leaf", None, "row"),
            P(),
        ),
        out_specs=(
            P("leaf", None, "row"),
            P("leaf", None, "row"),
            P("leaf", None, "row"),
            P("leaf", None, "row"),
        ),
        check_vma=False,
    )
```

profile of v0, /device:TPU:1, one launch (start us, length us, event | category | flops | bytes accessed | tf_op | source)
XLA Modules:
  0.0 404.3 jit_solution(16791441184361963141)
XLA Ops:
  8.1 1.7 bitcast_multiply_fusion.1
  16.1 39.5 %all-gather.9.cloned.1.call-done = bf16[512,2048]{1,0:T(8,128)(2,1)} async-done(((bf16[512,128]{1,0:T(8,128)(2,1)}), bf16[512,2048]{1,0:T(8,128)(2,1)}) %all-gather.9.cloned.1.call-update) | async-done | bytes 2097168 | tf_op jit(solution)/shard_map/all_gather | solution.py:27
  55.5 2.3 fusion.13
  57.8 48.6 %all-gather.11.cloned.1.call-done = f32[512,2048]{1,0:T(8,128)} async-done(((f32[512,128]{1,0:T(8,128)}), f32[512,2048]{1,0:T(8,128)}) %all-gather.11.cloned.1.call-update) | async-done | bytes 4194320 | tf_op jit(solution)/shard_map/all_gather | solution.py:19
  106.5 5.3 %copy.19 = f32[512,2048]{0,1:T(8,128)} copy(f32[512,2048]{1,0:T(8,128)} %all-gather.11.cloned.1.call-done) | data formatting | bytes 8388608 | tf_op jit(solution)/shard_map/all_gather | solution.py:19
  111.8 4.2 %gather_fusion.2 = f32[512,512]{1,0:T(8,128)S(1)} fusion(f32[512,2048]{0,1:T(8,128)} %copy.19, s32[1024]{0:T(1024)S(1)} %pad_clamp_fusion.1), kind=kCustom, calls=%fused_computation.clone | custom fusion | bytes 2099200 | tf_op jit(solution)/shard_map/jit(_take)/gather | solution.py:20
  116.0 1.9 convolution_negate_fusion.1
  118.6 3.9 convolution_subtract_fusion.1
  122.6 50.3 %all-gather.17.cloned.1.call-done = bf16[1,2048,2048]{2,1,0:T(8,128)(2,1)} async-done(((bf16[1,2048,128]{2,1,0:T(8,128)(2,1)}), bf16[1,2048,2048]{2,1,0:T(8,128)(2,1)}) %all-gather.17.cloned.1.call-update) | async-done | bytes 8388624 | tf_op jit(solution)/shard_map/all_gather | solution.py:34
  172.9 6.3 %fusion.2 = f32[128,2048]{1,0:T(8,128)S(1)} fusion(f32[2048,128]{1,0:T(8,128)S(1)} %convolution_subtract_fusion.1, bf16[1,2048,2048]{2,1,0:T(8,128)(2,1)} %all-gather.17.cloned.1.call-done), kind=kOutput, calls=%fused_computation.6 | convolution fusion | flops 6442450944 | bytes 10485760 | tf_op jit(solution)/shard_map/dot_general | solution.py:33
  179.5 27.8 %gather_fusion.1 = f32[8192,128]{1,0:T(8,128)} fusion(f32[2048,128]{1,0:T(8,128)S(1)} %copy.21, s32[8192]{0:T(1024)S(1)} %broadcast_clamp_fusion), kind=kCustom, calls=%fused_computation.3 | custom fusion | bytes 8421376 | tf_op jit(solution)/shard_map/jit(_take)/gather | solution.py:65
  207.3 5.3 %select_multiply_fusion = f32[16,512,128]{2,1,0:T(8,128)} fusion(f32[16,512,128]{2,1,0:T(8,128)} %bitcast.84, f32[16]{0:T(128)S(1)} %compare_convert_fusion, pred[16,512]{1,0:T(8,128)(4,1)S(1)} %compare_and_fusion), kind=kLoop, calls=%fused_computation.8 | loop fusion | flops 2097152 | bytes 8396864 | tf_op jit(solution)/shard_map/mul | solution.py:66
  212.5 4.7 %all-to-all-start = ((f32[16,512,128]{2,1,0:T(8,128)}), f32[16,512,128]{2,1,0:T(8,128)}, u32[]{:S(2)}, u32[]{:S(2)}) async-start(f32[16,512,128]{2,1,0:T(8,128)} %select_multiply_fusion), calls=%async_computation | async-start | bytes 8388608 | tf_op jit(solution)/shard_map/all_to_all | solution.py:67
  218.2 62.3 %all-to-all-done = f32[16,512,128]{2,1,0:T(8,128)} async-done(((f32[16,512,128]{2,1,0:T(8,128)}), f32[16,512,128]{2,1,0:T(8,128)}, u32[]{:S(2)}, u32[]{:S(2)}) %all-to-all-start) | async-done | bytes 4194336 | tf_op jit(solution)/shard_map/all_to_all | solution.py:67
  280.5 2.4 reduce_sum.9
  284.4 2.3 fusion.11
  286.7 1.3 copy.23
  288.0 35.5 %all-gather.15.cloned.1.call-done = f32[512,2048]{0,1:T(8,128)} async-done(((f32[512,128]{0,1:T(8,128)}), f32[512,2048]{0,1:T(8,128)}) %all-gather.15.cloned.1.call-update) | async-done | bytes 4194320 | tf_op jit(solution)/shard_map/all_gather | solution.py:19
  323.6 4.2 %gather_fusion.3 = f32[512,512]{1,0:T(8,128)S(1)} fusion(f32[512,2048]{0,1:T(8,128)} %all-gather.15.cloned.1.call-done, s32[1024]{0:T(1024)S(1)} %pad_clamp_fusion), kind=kCustom, calls=%fused_computation.1.clone | custom fusion | bytes 2099200 | tf_op jit(solution)/shard_map/jit(_take)/gather | solution.py:20
  327.8 1.9 convolution_negate_fusion
  329.7 4.0 convolution_subtract_fusion
  333.7 56.2 %all-gather.19.cloned.1.call-done = bf16[1,2048,2048]{2,1,0:T(8,128)(2,1)} async-done(((bf16[1,2048,128]{2,1,0:T(8,128)(2,1)}), bf16[1,2048,2048]{2,1,0:T(8,128)(2,1)}) %all-gather.19.cloned.1.call-update) | async-done | bytes 8388624 | tf_op jit(solution)/shard_map/all_gather | solution.py:34
  389.9 6.3 %fusion.4 = f32[1,2048,128]{1,2,0:T(8,128)S(1)} fusion(f32[2048,128]{1,0:T(8,128)S(1)} %convolution_subtract_fusion, bf16[1,2048,2048]{2,1,0:T(8,128)(2,1)} %all-gather.19.cloned.1.call-done), kind=kOutput, calls=%fused_computation.9 | convolution fusion | flops 6442450944 | bytes 10485760 | tf_op jit(solution)/shard_map/dot_general | solution.py:33
  396.2 1.3 copy.24
  (58 shorter events, 10.5 us)
Async XLA Ops:
  7.2 3.6 copy-start
  7.2 48.4 %copy-start.1 = (bf16[1,2048,128]{2,1,0:T(8,128)(2,1)S(1)}, bf16[1,2048,128]{2,1,0:T(8,128)(2,1)}, u32[]{:S(2)}) copy-start(bf16[1,2048,128]{2,1,0:T(8,128)(2,1)} %param.13) | copy-start | bytes 1572868
  7.2 48.3 %all-gather.9.cloned.1.call-start = ((), (), s32[]{:S(2)}) async-start(), calls=%async_computation.1 | async-start | bytes 2228224 | tf_op jit(solution)/shard_map/all_gather | solution.py:27
  9.8 96.7 %all-gather.11.cloned.1.call-start = ((), (), s32[]{:S(2)}) async-start(), calls=%async_computation.2 | async-start | bytes 4456448 | tf_op jit(solution)/shard_map/all_gather | solution.py:19
  12.8 160.1 %all-gather.17.cloned.1.call-start = ((), (), s32[]{:S(2)}) async-start(), calls=%async_computation.5 | async-start | bytes 8912896 | tf_op jit(solution)/shard_map/all_gather | solution.py:34
  117.9 0.7 copy-start.4
  212.5 4.8 %copy-start.6 = (bf16[1,512,128]{2,1,0:T(8,128)(2,1)S(1)}, bf16[1,512,128]{2,1,0:T(8,128)(2,1)}, u32[]{:S(2)}) copy-start(bf16[1,512,128]{2,1,0:T(8,128)(2,1)} %param.18) | copy-start | bytes 393220
  212.5 67.9 %all-to-all-start = ((f32[16,512,128]{2,1,0:T(8,128)}), f32[16,512,128]{2,1,0:T(8,128)}, u32[]{:S(2)}, u32[]{:S(2)}) async-start(f32[16,512,128]{2,1,0:T(8,128)} %select_multiply_fusion), calls=%async_computation | async-start | bytes 8388608 | tf_op jit(solution)/shard_map/all_to_all | solution.py:67
  217.2 67.2 %copy-start.2 = (bf16[1,2048,128]{2,1,0:T(8,128)(2,1)S(1)}, bf16[1,2048,128]{2,1,0:T(8,128)(2,1)}, u32[]{:S(2)}) copy-start(bf16[1,2048,128]{2,1,0:T(8,128)(2,1)} %param.17) | copy-start | bytes 1572868
  217.2 67.2 %all-gather.13.cloned.1.call-start = ((), (), s32[]{:S(2)}) async-start(), calls=%async_computation.3 | async-start | bytes 2228224 | tf_op jit(solution)/shard_map/all_gather | solution.py:27
  218.1 105.4 %all-gather.15.cloned.1.call-start = ((), (), s32[]{:S(2)}) async-start(), calls=%async_computation.4 | async-start | bytes 4456448 | tf_op jit(solution)/shard_map/all_gather | solution.py:19
  283.7 106.2 %all-gather.19.cloned.1.call-start = ((), (), s32[]{:S(2)}) async-start(), calls=%async_computation.6 | async-start | bytes 8912896 | tf_op jit(solution)/shard_map/all_gather | solution.py:34
  288.0 41.6 %copy-start.3 = (bf16[1,2048,128]{2,1,0:T(8,128)(2,1)S(1)}, bf16[1,2048,128]{2,1,0:T(8,128)(2,1)}, u32[]{:S(2)}) copy-start(bf16[1,2048,128]{2,1,0:T(8,128)(2,1)} %param.17) | copy-start | bytes 1572868
  329.7 4.0 copy-start.5
Sparse Core Ops, SparseCore 0:
  10.4 45.1 all-gather.8
  57.9 48.5 all-gather.10
  108.2 64.6 all-gather.16
  220.1 40.0 all-gather.12
  283.9 39.6 all-gather.14
  325.2 64.6 all-gather.18
where the time goes:
time: 405 us; the launch traced here: 404 us
  waiting for transfers between devices  294 us (73%)
  local copies, waits for them, and re-layouts  47.4 us (12%)
  matrix products  28.8 us (7%)
  other arithmetic  15.1 us (4%)
  between operations  14.4 us (4%)
  starting transfers between devices  5.12 us (1%)
    all_gather x2, waiting for transfers between devices, solve_block(): lax.all_gather(linv_local, 'row', axis=1, tiled=True).astype(jnp.float32)  107 us
    all_gather x2, waiting for transfers between devices, assemble(): gathered = lax.all_gather(selected, 'row', axis=1, tiled=True)  84.1 us
    all_to_all x1, waiting for transfers between devices, body(): lax.all_to_all(slots, 'leaf', split_axis=0, concat_axis=0, tiled=True)  62.3 us
    all_gather x2, waiting for transfers between devices, solve_block(): whole_panel = lax.all_gather(masked, 'row', axis=1, tiled=True)  39.5 us
    gather x1, local copies, waits for them, and re-layouts, body(): jnp.take(sigma_first, rows_every.reshape(-1), axis=0)  27.8 us
    dot_general x2, matrix products, solve_block(): jnp.dot(lax.all_gather(linv_local, 'row', axis=1, tiled=True).astype(jnp....  12.5 us
    gather x2, local copies, waits for them, and re-layouts, assemble(): return jnp.take(gathered, row_list, axis=1)  8.43 us
  transfers between devices with their start and end apart: 7, of which 6 were waited for; matrix products, arithmetic and copies ran while one was open for 10% of the time, Pallas kernels for 0%

commit v1 on v0

--- a/solution.py
+++ b/solution.py
@@ -1,9 +1,21 @@
+import functools
 import jax
 import jax.numpy as jnp
 from jax import lax
 from jax.sharding import PartitionSpec as P
 
 TILE = 128
+
+
+def proceed_slices(raw, net_axis, dim_i):
+    even = jnp.concatenate([raw for _ in range(lax.axis_size(net_axis))], dim_i)
+    q_next = lax.all_to_all(
+        even, axis_name=net_axis, split_axis=dim_i, tiled=True, concat_axis=dim_i
+    )
+    return q_next
+
+
+bring_ranges = functools.partial(proceed_slices, net_axis="row", dim_i=1)
 
 
 def pattern_rows(tile_list):
@@ -24,7 +36,7 @@
     select = assemble(selected, row_list)
     masked = panel_local * expand_mask(mask_local).astype(jnp.bfloat16)
     linv_wide = linv_local.astype(jnp.float32)
-    whole_panel = lax.all_gather(masked, "row", axis=1, tiled=True)
+    whole_panel = bring_ranges(masked)
     upper_part = jnp.dot(whole_panel, linv_local, preferred_element_type=jnp.float32)
     cross = -jnp.dot(select, upper_part, precision=lax.Precision.HIGHEST)
     middle = linv_wide - jnp.dot(

time: 405 us -> 422 us (1.042)
  blocking collectives: 0 us -> 54.4 us
  waiting for transfers between devices: 294 us -> 242 us
  starting transfers between devices: 5.12 us -> 16.4 us
  local copies, waits for them, and re-layouts: 47.4 us -> 57.5 us
  other arithmetic: 15.1 us -> 10.1 us
    all_gather x2, waiting for transfers between devices: 84.1 us -> 12.5 us  [assemble(): gathered = lax.all_gather(selected, 'row', axis=1, tiled=True)]
    all_to_all x1 -> x2, waiting for transfers between devices: 62.3 us -> 125 us  [proceed_slices(): lax.all_to_all(even, axis_name=net_axis, split_axis=dim_i, tiled=True, co...]
    all_to_all x0 -> x1, blocking collectives: none -> 54.4 us  [body(): lax.all_to_all(slots, 'leaf', split_axis=0, concat_axis=0, tiled=True)]
    all_gather x2 -> x0, waiting for transfers between devices: 39.5 us -> none  [solve_block(): whole_panel = lax.all_gather(masked, 'row', axis=1, tiled=True)]
    all_to_all x1 -> x2, starting transfers between devices: 4.69 us -> 16.3 us  [proceed_slices(): lax.all_to_all(even, axis_name=net_axis, split_axis=dim_i, tiled=True, co...]
    all_to_all x0 -> x2, local copies, waits for them, and re-layouts: none -> 5.73 us  [proceed_slices(): lax.all_to_all(even, axis_name=net_axis, split_axis=dim_i, tiled=True, co...]
  transfers between devices with their start and end apart: 7 -> 6, of which waited for: 6 -> 5; matrix products, arithmetic and copies ran while one was open for 10% -> 10% of each run, Pallas kernels for 0% -> 0%
where the time goes in v1:
time: 422 us; the launch traced here: 421 us
  waiting for transfers between devices  242 us (57%)
  local copies, waits for them, and re-layouts  57.5 us (14%)
  blocking collectives  54.4 us (13%)
  matrix products  26.1 us (6%)
  starting transfers between devices  16.4 us (4%)
  between operations  14.1 us (3%)
  other arithmetic  10.1 us (2%)
    all_to_all x2, waiting for transfers between devices, proceed_slices(): lax.all_to_all(even, axis_name=net_axis, split_axis=dim_i, tiled=True, co...  125 us
    all_gather x2, waiting for transfers between devices, solve_block(): lax.all_gather(linv_local, 'row', axis=1, tiled=True).astype(jnp.float32)  104 us
    all_to_all x1, blocking collectives, body(): lax.all_to_all(slots, 'leaf', split_axis=0, concat_axis=0, tiled=True)  54.4 us
    gather x1, local copies, waits for them, and re-layouts, body(): jnp.take(sigma_first, rows_every.reshape(-1), axis=0)  27.9 us
    all_to_all x2, starting transfers between devices, proceed_slices(): lax.all_to_all(even, axis_name=net_axis, split_axis=dim_i, tiled=True, co...  16.3 us
    dot_general x2, matrix products, solve_block(): jnp.dot(lax.all_gather(linv_local, 'row', axis=1, tiled=True).astype(jnp....  12.9 us
    all_gather x2, waiting for transfers between devices, assemble(): gathered = lax.all_gather(selected, 'row', axis=1, tiled=True)  12.5 us
    gather x2, local copies, waits for them, and re-layouts, assemble(): return jnp.take(gathered, row_list, axis=1)  9.18 us
  transfers between devices with their start and end apart: 6, of which 5 were waited for; matrix products, arithmetic and copies ran while one was open for 10% of the time, Pallas kernels for 0%

profile of v1, /device:TPU:1, one launch (start us, length us, event | category | flops | bytes accessed | tf_op | source)
XLA Modules:
  0.0 421.0 jit_solution(16666683376809430414)
XLA Ops:
  12.9 1.7 concatenate.8
  14.6 10.1 %all-to-all-start = ((bf16[512,16,128]{2,0,1:T(8,128)(2,1)}), bf16[512,16,128]{2,0,1:T(8,128)(2,1)}, u32[]{:S(2)}, u32[]{:S(2)}) async-start(bf16[512,16,128]{2,0,1:T(8,128)(2,1)} %concatenate.8), calls=%async_computation | async-start | bytes 4194304 | tf_op jit(solution)/shard_map/all_to_all | solution.py:12
  25.2 59.7 %all-to-all-done = bf16[512,16,128]{2,0,1:T(8,128)(2,1)} async-done(((bf16[512,16,128]{2,0,1:T(8,128)(2,1)}), bf16[512,16,128]{2,0,1:T(8,128)(2,1)}, u32[]{:S(2)}, u32[]{:S(2)}) %all-to-all-start) | async-done | bytes 2097184 | tf_op jit(solution)/shard_map/all_to_all | solution.py:12
  84.9 2.9 copy.25
  88.5 12.5 %all-gather.7.cloned.1.call-done = f32[512,2048]{1,0:T(8,128)} async-done(((f32[512,128]{1,0:T(8,128)}), f32[512,2048]{1,0:T(8,128)}) %all-gather.7.cloned.1.call-update) | async-done | bytes 4194320 | tf_op jit(solution)/shard_map/all_gather | solution.py:31
  101.0 5.3 %copy.26 = f32[512,2048]{0,1:T(8,128)} copy(f32[512,2048]{1,0:T(8,128)} %all-gather.7.cloned.1.call-done) | data formatting | bytes 8388608 | tf_op jit(solution)/shard_map/all_gather | solution.py:31
  106.3 4.2 %gather_fusion.2 = f32[512,512]{1,0:T(8,128)S(1)} fusion(f32[512,2048]{0,1:T(8,128)} %copy.26, s32[1024]{0:T(1024)S(1)} %pad_clamp_fusion.1), kind=kCustom, calls=%fused_computation.clone | custom fusion | bytes 2099200 | tf_op jit(solution)/shard_map/jit(_take)/gather | solution.py:32
  110.6 1.9 convolution_negate_fusion.1
  113.2 2.9 convolution_subtract_fusion.1
  116.0 51.9 %all-gather.11.cloned.1.call-done = bf16[1,2048,2048]{2,1,0:T(8,128)(2,1)} async-done(((bf16[1,2048,128]{2,1,0:T(8,128)(2,1)}), bf16[1,2048,2048]{2,1,0:T(8,128)(2,1)}) %all-gather.11.cloned.1.call-update) | async-done | bytes 8388624 | tf_op jit(solution)/shard_map/all_gather | solution.py:46
  167.9 6.3 %fusion.2 = f32[128,2048]{1,0:T(8,128)S(1)} fusion(f32[2048,128]{1,0:T(8,128)S(1)} %convolution_subtract_fusion.1, bf16[1,2048,2048]{2,1,0:T(8,128)(2,1)} %all-gather.11.cloned.1.call-done), kind=kOutput, calls=%fused_computation.6 | convolution fusion | flops 6442450944 | bytes 10485760 | tf_op jit(solution)/shard_map/dot_general | solution.py:45
  174.5 27.9 %gather_fusion.1 = f32[8192,128]{1,0:T(8,128)} fusion(f32[2048,128]{1,0:T(8,128)S(1)} %copy.29, s32[8192]{0:T(1024)S(1)} %broadcast_clamp_fusion), kind=kCustom, calls=%fused_computation.3 | custom fusion | bytes 8421376 | tf_op jit(solution)/shard_map/jit(_take)/gather | solution.py:77
  202.4 3.6 select_multiply_fusion
  206.0 54.4 %all_to_all.23 = f32[16,512,128]{2,1,0:T(8,128)} all-to-all(f32[16,512,128]{2,1,0:T(8,128)S(1)} %select_multiply_fusion), channel_id=1, replica_groups=mesh['leaf'=16,'row'=16] {'leaf'}, dimensions={0} | all-to-all | bytes 8388608 | tf_op jit(solution)/shard_map/all_to_all | solution.py:79
  260.4 2.5 reduce_sum.9
  266.2 6.2 %all-to-all-start.1 = ((bf16[512,16,128]{2,0,1:T(8,128)(2,1)}), bf16[512,16,128]{2,0,1:T(8,128)(2,1)}, u32[]{:S(2)}, u32[]{:S(2)}) async-start(bf16[512,16,128]{2,0,1:T(8,128)(2,1)} %concatenate.9), calls=%async_computation.1 | async-start | bytes 4194304 | tf_op jit(solution)/shard_map/all_to_all | solution.py:12
  272.5 65.5 %all-to-all-done.1 = bf16[512,16,128]{2,0,1:T(8,128)(2,1)} async-done(((bf16[512,16,128]{2,0,1:T(8,128)(2,1)}), bf16[512,16,128]{2,0,1:T(8,128)(2,1)}, u32[]{:S(2)}, u32[]{:S(2)}) %all-to-all-start.1) | async-done | bytes 2097184 | tf_op jit(solution)/shard_map/all_to_all | solution.py:12
  338.0 2.9 copy.27
  340.8 1.8 fusion.11
  343.9 5.0 %gather_fusion.3 = f32[512,512]{1,0:T(8,128)} fusion(f32[512,2048]{0,1:T(8,128)} %all-gather.9.cloned.1.call-done, s32[1024]{0:T(1024)S(1)} %pad_clamp_fusion), kind=kCustom, calls=%fused_computation.1.clone | custom fusion | bytes 2099200 | tf_op jit(solution)/shard_map/jit(_take)/gather | solution.py:32
  348.9 3.1 convolution_negate_fusion
  352.0 2.8 convolution_subtract_fusion
  354.8 51.6 %all-gather.13.cloned.1.call-done = bf16[1,2048,2048]{2,1,0:T(8,128)(2,1)} async-done(((bf16[1,2048,128]{2,1,0:T(8,128)(2,1)}), bf16[1,2048,2048]{2,1,0:T(8,128)(2,1)}) %all-gather.13.cloned.1.call-update) | async-done | bytes 8388624 | tf_op jit(solution)/shard_map/all_gather | solution.py:46
  406.5 6.6 %fusion.4 = f32[1,2048,128]{1,2,0:T(8,128)S(1)} fusion(f32[2048,128]{1,0:T(8,128)} %convolution_subtract_fusion, bf16[1,2048,2048]{2,1,0:T(8,128)(2,1)} %all-gather.13.cloned.1.call-done), kind=kOutput, calls=%fused_computation.9 | convolution fusion | flops 6442450944 | bytes 10485760 | tf_op jit(solution)/shard_map/dot_general | solution.py:45
  (69 shorter events, 13.9 us)
Async XLA Ops:
  7.2 1.2 copy-start
  7.2 93.8 %all-gather.7.cloned.1.call-start = ((), (), s32[]{:S(2)}) async-start(), calls=%async_computation.3 | async-start | bytes 4456448 | tf_op jit(solution)/shard_map/all_gather | solution.py:31
  9.4 15.3 %copy-start.9 = (s32[16,4]{0,1:T(4,128)S(1)}, s32[16,4]{0,1:T(4,128)}, u32[]{:S(2)}) copy-start(s32[16,4]{0,1:T(4,128)} %param.19) | copy-start | bytes 772
  9.5 15.5 %copy-start.10 = (s32[16]{0:T(128)S(1)}, s32[16]{0:T(128)}, u32[]{:S(2)}) copy-start(s32[16]{0:T(128)} %param.21) | copy-start | bytes 196
  10.3 157.6 %all-gather.11.cloned.1.call-start = ((), (), s32[]{:S(2)}) async-start(), calls=%async_computation.5 | async-start | bytes 8912896 | tf_op jit(solution)/shard_map/all_gather | solution.py:46
  14.6 73.2 %copy-start.4 = (bf16[1,2048,128]{2,1,0:T(8,128)(2,1)S(1)}, bf16[1,2048,128]{2,1,0:T(8,128)(2,1)}, u32[]{:S(2)}) copy-start(bf16[1,2048,128]{2,1,0:T(8,128)(2,1)} %param.13) | copy-start | bytes 1572868
  14.6 70.3 %all-to-all-start = ((bf16[512,16,128]{2,0,1:T(8,128)(2,1)}), bf16[512,16,128]{2,0,1:T(8,128)(2,1)}, u32[]{:S(2)}, u32[]{:S(2)}) async-start(bf16[512,16,128]{2,0,1:T(8,128)(2,1)} %concatenate.8), calls=%async_computation | async-start | bytes 4194304 | tf_op jit(solution)/shard_map/all_to_all | solution.py:12
  24.7 319.2 %all-gather.9.cloned.1.call-start = ((), (), s32[]{:S(2)}) async-start(), calls=%async_computation.4 | async-start | bytes 4456448 | tf_op jit(solution)/shard_map/all_gather | solution.py:31
  112.5 0.7 copy-start.6
  174.2 28.2 %copy-start.2 = (f32[128,2048]{1,0:T(8,128)}, f32[128,2048]{1,0:T(8,128)S(1)}, u32[]{:S(2)}) copy-start(f32[128,2048]{1,0:T(8,128)S(1)} %fusion.2) | copy-start | bytes 3145732
  260.4 3.9 copy-start.11
  260.4 4.0 copy-start.8
  263.7 142.8 %all-gather.13.cloned.1.call-start = ((), (), s32[]{:S(2)}) async-start(), calls=%async_computation.6 | async-start | bytes 8912896 | tf_op jit(solution)/shard_map/all_gather | solution.py:46
  266.2 71.7 %all-to-all-start.1 = ((bf16[512,16,128]{2,0,1:T(8,128)(2,1)}), bf16[512,16,128]{2,0,1:T(8,128)(2,1)}, u32[]{:S(2)}, u32[]{:S(2)}) async-start(bf16[512,16,128]{2,0,1:T(8,128)(2,1)} %concatenate.9), calls=%async_computation.1 | async-start | bytes 4194304 | tf_op jit(solution)/shard_map/all_to_all | solution.py:12
  272.4 70.2 %copy-start.3 = (f32[128,2048]{1,0:T(8,128)S(1)}, f32[128,2048]{1,0:T(8,128)}, u32[]{:S(2)}) copy-start(f32[128,2048]{1,0:T(8,128)} %copy-done.2) | copy-start | bytes 3145732
  343.9 8.1 %copy-start.5 = (bf16[1,2048,128]{2,1,0:T(8,128)(2,1)S(1)}, bf16[1,2048,128]{2,1,0:T(8,128)(2,1)}, u32[]{:S(2)}) copy-start(bf16[1,2048,128]{2,1,0:T(8,128)(2,1)} %param.17) | copy-start | bytes 1572868
  352.0 2.8 copy-start.7
  406.5 8.0 %copy-start.1 = (f32[2048,128]{1,0:T(8,128)S(1)}, f32[2048,128]{1,0:T(8,128)}, u32[]{:S(2)}) copy-start(f32[2048,128]{1,0:T(8,128)} %param.12) | copy-start | bytes 3145732
Sparse Core Ops, SparseCore 0:
  10.5 90.5 all-gather.6
  102.8 65.1 all-gather.10
  263.8 77.4 all-gather.8
  343.0 63.4 all-gather.12
